TPU v7x, 256 devices: a whole 4x4x8 slice. The times are simulated.
256 devices in a mesh: ctx: 32 (over y, z_lo, core), ch: 8 (over z_hi, x).
Axes of the slice: x: 4, y: 4, z: 8 (z_hi: 2, z_lo: 4; z = z_hi * 4 + z_lo), core: 2. Of those that a mesh axis runs over, the one named last changes fastest.
Arguments:
- token_ids: int32 [16384], P('ctx'), may hold values from 65 to 84, as said below
- embedding: bfloat16 [512, 4096], P(None, 'ch'), may hold values from -6 to 6
- long_table: bfloat16 [512, 3, 4096], P(None, None, 'ch'), may hold values from -6 to 6
- long_taps: float32 [3, 3, 4096], P(None, None, 'ch'), may hold values from -3 to 3
- long_residue: float32 [256, 16], P('ch'), may hold values from -1.5 to 1.5
- long_rate: float32 [256, 16], P('ch'), may hold values from 1.2207031e-06 to 0.04
- long_skip: float32 [4096], P('ch'), may hold values from 0.25 to 1.75
- medium_gain: bfloat16 [4096], P('ch'), may hold values from 0.25 to 1.75
- medium_weight: bfloat16 [4096, 3, 4096], P('ctx', None, 'ch'), may hold values from -0.09375 to 0.09375
- medium_taps: float32 [3, 3, 4096], P(None, None, 'ch'), may hold values from -3 to 3
- medium_group_filter: float32 [256, 128], P('ch'), may hold values from -0.6 to 0.6
- medium_skip: float32 [4096], P('ch'), may hold values from 0.25 to 1.75
- filter_group: int32 [4096], P('ch'), may hold values from 0 to 255, as said below
Outputs:
- block_output: bfloat16 [16384, 4096], P('ctx', 'ch')
Inputs may be any that keep to these rules, and one draw needn't show every extreme that they name: `token_ids`: every token is the byte code of A, C, G, T or N. `filter_group`: each filter group has exactly 16 channels, all within one block of 512 consecutive channels; block j holds groups j * (32) to (j + 1) * 32 - 1.
All inputs are finite; a program needn't handle non-finite values.
Results may differ from a plain program's by a relative error of at most 0.006.
Values may be sent and summed in bfloat16 or wider, within the bound.
A program may use at most 128 MiB of HBM per device.

v0:
```python
import jax
import jax.numpy as jnp
from jax import lax
from jax.sharding import PartitionSpec as P

MODEL_WIDTH = 4096
epsilon = 1e-06


def from_behind(x, axis, by):
    count = lax.axis_size(axis)
    pairs = [(i, i + by) for i in range(count) if 0 <= i + by < count]
    return lax.ppermute(x, axis, pairs)


def carried_in(value, axis, join, neutral):
    count, mine = (lax.axis_size(axis), lax.axis_index(axis))
    pieces = jax.tree.map(lambda part: lax.all_gather(part, axis), value)
    running = jax.tree.map(
        lambda part, zero: jnp.full_like(part, 0) + jnp.asarray(zero, part.dtype), value, neutral
    )

    def turn(position, running):
        longer = join(running, jax.tree.map(lambda part: part[position], pieces))
        return jax.tree.map(lambda new, old: jnp.where(position < mine, new, old), longer, running)

    return lax.fori_loop(0, count - 1, turn, running)


def featurize(streams, before, filter_taps):
    extended = jnp.concatenate([before, streams], axis=0).astype(jnp.float32)
    length = streams.shape[0]
    mixed = filter_taps[0] * extended[2 : 2 + length]
    mixed = mixed + filter_taps[1] * extended[1 : 1 + length]
    mixed = mixed + filter_taps[2] * extended[0:length]
    return mixed


def previous_rows(values, count):
    return from_behind(values[values.shape[0] - count :], "ctx", 1)


def chain_combine(earlier, later):
    return (earlier[0] * later[0], earlier[1] * later[0] + later[1])


def split_product(form, data, table):
    upper = table.astype(jnp.bfloat16)
    lower = (table - upper.astype(jnp.float32)).astype(jnp.bfloat16)
    first = jnp.einsum(form, data, upper, preferred_element_type=jnp.float32)
    return first + jnp.einsum(form, data, lower, preferred_element_type=jnp.float32)


def local(
    token_ids,
    embedding,
    long_table,
    long_taps,
    long_residue,
    long_rate,
    long_skip,
    medium_gain,
    medium_weight,
    medium_taps,
    medium_group_filter,
    medium_skip,
    filter_group,
):
    tokens = token_ids.shape[0]
    channels = embedding.shape[1]
    vocab = embedding.shape[0]
    groups = long_rate.shape[0]
    pole_count = long_rate.shape[1]
    tap_count = medium_group_filter.shape[1]
    members = channels // groups
    blocks = tokens // tap_count
    one_hot = (token_ids[:, None] == jnp.arange(vocab, dtype=jnp.int32)[None, :]).astype(
        jnp.bfloat16
    )
    resid = jnp.dot(one_hot, embedding, preferred_element_type=jnp.float32)
    streams = jnp.dot(
        one_hot, long_table.reshape(vocab, 3 * channels), preferred_element_type=jnp.float32
    )
    streams = streams.astype(jnp.bfloat16).reshape(tokens, 3, channels)
    local_group = filter_group - lax.axis_index("ch") * groups
    channel_ids = jnp.arange(channels, dtype=jnp.int32)
    same_group = local_group[:, None] == local_group[None, :]
    rank_within = jnp.sum(same_group & (channel_ids[None, :] < channel_ids[:, None]), axis=1)
    placed = local_group * members + rank_within
    select = placed[:, None] == channel_ids[None, :]
    select_half = select.astype(jnp.bfloat16)
    select_wide = select.astype(jnp.float32)

    def grouped(values):
        length = values.shape[0]
        moved = jnp.dot(values, select_half, preferred_element_type=jnp.float32).astype(
            jnp.bfloat16
        )
        return moved.reshape(length, groups, members).transpose(1, 2, 0)

    def ungrouped(values):
        length = values.shape[-1]
        flat = values.transpose(2, 0, 1).reshape(length, channels)
        return jnp.dot(
            flat, select_wide.T, precision=lax.Precision.HIGHEST, preferred_element_type=jnp.float32
        )

    before = previous_rows(streams, 2)
    mixed = featurize(streams, before, long_taps)
    query = mixed[:, 0]
    product = (mixed[:, 1] * mixed[:, 2]).astype(jnp.bfloat16)
    product_wide = product.astype(jnp.float32)
    positions = jnp.arange(tap_count, dtype=jnp.float32)
    weight_res = long_residue * jnp.sqrt(-jnp.expm1(-2.0 * long_rate))
    kernel = jnp.sum(weight_res[:, :, None] * jnp.exp(-long_rate[:, :, None] * positions), axis=1)
    offsets = jnp.arange(tap_count, dtype=jnp.int32)
    lag = offsets[None, :] - offsets[:, None]
    toeplitz = jnp.where(lag[None] >= 0, kernel[:, jnp.clip(lag, 0, tap_count - 1)], 0.0)
    blocked = grouped(product).reshape(groups, members, blocks, tap_count)
    inner = split_product("gcns,gst->gcnt", blocked, toeplitz)
    ending = jnp.exp(-long_rate[:, :, None] * (tap_count - 1.0 - positions))
    closing = split_product("gcns,gps->gcnp", blocked, ending)
    across = jnp.exp(-long_rate * tap_count)[:, None, :]
    summary = jnp.zeros((groups, members, pole_count), jnp.float32)
    for block in range(blocks):
        summary = summary * across + closing[:, :, block]
    whole_decay = jnp.broadcast_to(
        jnp.exp(-long_rate * tokens)[:, None, :], (groups, members, pole_count)
    )
    decay_flat = whole_decay.transpose(2, 0, 1).reshape(pole_count, channels)
    summary_flat = summary.transpose(2, 0, 1).reshape(pole_count, channels)
    identity = (
        jnp.ones((pole_count, channels), jnp.float32),
        jnp.zeros((pole_count, channels), jnp.float32),
    )
    carried = carried_in((decay_flat, summary_flat), "ctx", chain_combine, identity)[1]
    state = carried.reshape(pole_count, groups, members).transpose(1, 2, 0)
    starts = []
    for block in range(blocks):
        starts.append(state)
        state = state * across + closing[:, :, block]
    start_stack = jnp.stack(starts, axis=2)
    entry = weight_res[:, :, None] * jnp.exp(-long_rate[:, :, None] * (positions + 1.0))
    outer = jnp.einsum("gcnp,gpt->gcnt", start_stack, entry, precision=lax.Precision.HIGHEST)
    conv_long = (
        ungrouped((inner + outer).reshape(groups, members, tokens)) + long_skip * product_wide
    )
    middle = (resid + query * conv_long).astype(jnp.bfloat16)
    middle_wide = middle.astype(jnp.float32)
    squares = lax.psum(jnp.sum(middle_wide * middle_wide, axis=1), "ch")
    scale = lax.rsqrt(squares / MODEL_WIDTH + epsilon)
    normed = (middle_wide * scale[:, None] * medium_gain.astype(jnp.float32)).astype(jnp.bfloat16)
    features = lax.all_gather(normed, "ch", axis=1, tiled=True)
    piece = lax.all_gather(medium_weight, "ctx", axis=0, tiled=True)
    projected = jnp.dot(
        features, piece.reshape(piece.shape[0], 3 * channels), preferred_element_type=jnp.float32
    )
    projected = projected.astype(jnp.bfloat16).reshape(tokens, 3, channels)
    before2 = previous_rows(projected, 2)
    mixed2 = featurize(projected, before2, medium_taps)
    product2 = (mixed2[:, 1] * mixed2[:, 2]).astype(jnp.bfloat16)
    margin = previous_rows(product2, tap_count)
    query2 = mixed2[:, 0]
    second_product_wide = product2.astype(jnp.float32)
    extended = jnp.concatenate([margin, product2], axis=0)
    framed = grouped(extended).reshape(groups, members, blocks + 1, tap_count)
    windows = jnp.concatenate([framed[:, :, :-1], framed[:, :, 1:]], axis=-1)
    wide_offsets = jnp.arange(2 * tap_count, dtype=jnp.int32)
    tap_delay = offsets[None, :] + tap_count - wide_offsets[:, None]
    valid = (tap_delay >= 0) & (tap_delay < tap_count)
    banded = jnp.where(
        valid[None], medium_group_filter[:, jnp.clip(tap_delay, 0, tap_count - 1)], 0.0
    )
    medium = split_product("gcns,gst->gcnt", windows, banded)
    medium_convolution = (
        ungrouped(medium.reshape(groups, members, tokens)) + medium_skip * second_product_wide
    )
    return (middle_wide + query2 * medium_convolution).astype(jnp.bfloat16)


def solution(mesh):
    in_specs = (
        P("ctx"),
        P(None, "ch"),
        P(None, None, "ch"),
        P(None, None, "ch"),
        P("ch", None),
        P("ch", None),
        P("ch"),
        P("ch"),
        P("ctx", None, "ch"),
        P(None, None, "ch"),
        P("ch", None),
        P("ch"),
        P("ch"),
    )
    out_specs = P("ctx", "ch")
    return jax.shard_map(local, mesh=mesh, in_specs=in_specs, out_specs=out_specs, check_vma=False)
```

profile of v0, /device:TPU:8, one launch (start us, length us, event | category | flops | bytes accessed | tf_op | source)
XLA Modules:
  0.0 565.7 jit_solution(1877062003630645721)
XLA Ops:
  6.5 1.8 copy.92
  8.4 1.0 convolution_convert_fusion.1
  9.4 1.2 copy-done.10
  10.9 1.9 collective-permute-start
  14.1 1.7 copy.94
  16.1 6.6 %collective-permute-done = bf16[2,3,512]{0,2,1:T(8,128)(2,1)S(1)} collective-permute-done((bf16[2,3,512]{0,2,1:T(8,128)(2,1)S(1)}, bf16[2,3,512]{0,2,1:T(8,128)(2,1)S(1)}, u32[]{:S(2)}, u32[]{:S(2)}) %collective-permute-start) | collective-permute-done | bytes 6176 | tf_op jit(solution)/shard_map/ppermute | solution.py:13
  22.7 0.9 maximum_convert_fusion
  23.5 2.8 fusion.4
  28.3 0.9 copy-done.5
  30.4 54.5 %gather_fusion = f32[16384,32]{1,0:T(8,128)} fusion(f32[32,128]{0,1:T(8,128)S(1)} %copy.97, s32[16384]{0:T(1024)S(1)} %fusion.91), kind=kCustom, calls=%fused_computation | custom fusion | bytes 4259840 | tf_op jit(solution)/shard_map/gather | solution.py:118
  84.9 5.6 copy.98
  90.6 1.6 fusion.44
  92.2 1.4 fusion.26
  93.6 42.2 %all-gather.7.cloned.1.call-done = f32[32,16,512]{2,1,0:T(8,128)} async-done(((f32[1,16,512]{2,1,0:T(8,128)}), f32[32,16,512]{2,1,0:T(8,128)}) %all-gather.7.cloned.1.call-update) | async-done | bytes 1048592 | tf_op jit(solution)/shard_map/all_gather | solution.py:18
  135.7 25.2 %while.14 = (s32[]{:T(128)}, f32[16,512]{1,0:T(8,128)S(1)}, s32[]{:T(128)}, f32[32,16,512]{2,1,0:T(8,128)}, f32[32,16,512]{2,1,0:T(8,128)}, /*index=5*/s32[]{:T(128)}, s32[]{:T(128)}) while((s32[]{:T(128)}, f32[16,512]{1,0:T(8,128)S(1)}, s32[]{:T(128)}, f32[32,16,512]{2,1,0:T(8,128)}, f32[32,16,512]{2,1,0:T(8,128)}, ...), condition=%wide.region_3.4_spmd.clone, body=%wide.region_2.3_spmd.clone.sunk | while | flops 32772 | bytes 131173 | solution.py:27
  136.5 0.8 fusion.110
  137.4 0.8 fusion.110
  138.2 0.8 fusion.110
  139.0 0.8 fusion.110
  139.8 0.8 fusion.110
  140.6 0.8 fusion.110
  141.4 0.8 fusion.110
  142.2 0.8 fusion.110
  143.0 0.8 fusion.110
  143.9 0.8 fusion.110
  144.7 0.8 fusion.110
  145.5 0.8 fusion.110
  146.3 0.8 fusion.110
  147.1 0.8 fusion.110
  147.9 0.8 fusion.110
  148.7 0.8 fusion.110
  149.5 0.8 fusion.110
  150.4 0.8 fusion.110
  151.2 0.8 fusion.110
  152.0 0.8 fusion.110
  152.8 0.8 fusion.110
  153.6 0.8 fusion.110
  154.4 0.8 fusion.110
  155.2 0.8 fusion.110
  156.0 0.8 fusion.110
  156.9 0.8 fusion.110
  157.7 0.8 fusion.110
  158.5 0.8 fusion.110
  161.0 1.3 fusion.89
  162.3 1.1 fusion.40
  164.8 2.6 fusion.28
  167.4 29.8 %psum.7 = f32[512]{0:T(512)S(1)} all-reduce(f32[512]{0:T(512)S(1)} %get-tuple-element.144), channel_id=1, replica_groups=mesh['ctx'=32,'ch'=8] {'ch'}, use_global_device_ids=true, to_apply=%region_5.6 | all-reduce | flops 512 | bytes 4096 | tf_op jit(solution)/shard_map/psum | solution.py:150
  197.2 0.9 fusion.30
  198.4 0.9 copy.112
  199.5 100.5 %all-gather.9.cloned.1.call-done = bf16[512,4096]{0,1:T(8,128)(2,1)} async-done(((bf16[512,512]{0,1:T(8,128)(2,1)}), bf16[512,4096]{0,1:T(8,128)(2,1)}) %all-gather.9.cloned.1.call-update) | async-done | bytes 4194320 | tf_op jit(solution)/shard_map/all_gather | solution.py:153
  300.0 101.1 %all-gather.11.cloned.1.call-done = bf16[4096,3,512]{0,2,1:T(8,128)(2,1)} async-done(((bf16[128,3,512]{0,2,1:T(8,128)(2,1)}), bf16[4096,3,512]{0,2,1:T(8,128)(2,1)}) %all-gather.11.cloned.1.call-update) | async-done | bytes 12582928 | tf_op jit(solution)/shard_map/all_gather | solution.py:154
  401.1 11.0 %convolution_convert_fusion = bf16[512,1536]{1,0:T(8,128)(2,1)S(1)} fusion(bf16[512,4096]{0,1:T(8,128)(2,1)} %all-gather.9.cloned.1.call-done, bf16[4096,1536]{0,1:T(8,128)(2,1)} %bitcast.244), kind=kOutput, calls=%fused_computation.18 | convolution fusion | flops 6443237376 | bytes 18350080 | tf_op jit(solution)/shard_map/dot_general | solution.py:155
  412.1 1.2 copy-done.11
  413.5 2.2 collective-permute-start.1
  415.8 108.5 %gather_fusion.1 = f32[32768,32]{1,0:T(8,128)} fusion(f32[32,128]{0,1:T(8,128)S(1)} %copy.117, s32[32768]{0:T(1024)S(1)} %fusion.78), kind=kCustom, calls=%fused_computation.1 | custom fusion | bytes 8519680 | tf_op jit(solution)/shard_map/gather | solution.py:172
  524.3 11.8 %copy.118 = f32[256,128,32]{1,0,2:T(8,128)} copy(f32[256,128,32]{2,1,0:T(8,128)} %bitcast.227) | data formatting | bytes 8388608 | tf_op jit(solution)/shard_map/gather | solution.py:172
  536.1 1.7 copy.114
  537.8 0.9 maximum_convert_fusion.1
  538.7 2.8 fusion.2
  541.6 3.4 collective-permute-start.2
  545.2 5.5 collective-permute-done.2
  552.8 1.5 copy-done.2
  555.7 2.4 fusion.31
  558.1 1.0 copy.121
  (104 shorter events, 13.3 us)
Async XLA Ops:
  6.5 84.0 %copy-start = (bf16[512,512]{1,0:T(8,128)(2,1)S(1)}, bf16[512,512]{1,0:T(8,128)(2,1)}, u32[]{:S(2)}) copy-start(bf16[512,512]{1,0:T(8,128)(2,1)} %param.16) | copy-start | bytes 1572868
  6.5 1.8 copy-start.19
  6.5 87.0 %all-gather.5.cloned.1.call-start = ((), (), s32[]{:S(2)}) async-start(), calls=%async_computation | async-start | bytes 1081344 | tf_op jit(solution)/shard_map/all_gather | solution.py:18
  8.3 4.5 copy-start.16
  8.3 4.5 copy-start.17
  8.4 5.5 copy-start.13
  8.4 5.5 copy-start.18
  9.4 1.2 copy-start.10
  10.9 11.8 %collective-permute-start = (bf16[2,3,512]{0,2,1:T(8,128)(2,1)S(1)}, bf16[2,3,512]{0,2,1:T(8,128)(2,1)S(1)}, u32[]{:S(2)}, u32[]{:S(2)}) collective-permute-start(bf16[2,3,512]{0,2,1:T(8,128)(2,1)S(1)} %bitcast.242), channel_id=1, source_target_pairs={{0,8},{8,16},{16,24},{24,32},{32,40},{40,48},{48,56},{56,64},{64,7... | collective-permute-start | bytes 18440 | tf_op jit(solution)/shard_map/ppermute | solution.py:13
  13.8 122.0 %all-gather.7.cloned.1.call-start = ((), (), s32[]{:S(2)}) async-start(), calls=%async_computation.1 | async-start | bytes 1081344 | tf_op jit(solution)/shard_map/all_gather | solution.py:18
  26.3 1.9 copy-start.4
  26.5 1.0 copy-start.8
  28.2 1.0 copy-start.5
  29.9 270.1 %all-gather.9.cloned.1.call-start = ((), (), s32[]{:S(2)}) async-start(), calls=%async_computation.2 | async-start | bytes 4718592 | tf_op jit(solution)/shard_map/all_gather | solution.py:153
  84.9 5.6 copy-start.22
  161.0 2.4 copy-start.7
  163.5 1.2 copy-start.6
  163.5 1.3 copy-start.9
  163.5 1.3 copy-start.20
  164.1 34.3 %copy-start.12 = (bf16[128,3,512]{2,0,1:T(8,128)(2,1)S(1)}, bf16[128,3,512]{2,0,1:T(8,128)(2,1)}, u32[]{:S(2)}) copy-start(bf16[128,3,512]{2,0,1:T(8,128)(2,1)} %param.23) | copy-start | bytes 1179652
  198.2 202.9 %all-gather.11.cloned.1.call-start = ((), (), s32[]{:S(2)}) async-start(), calls=%async_computation.3 | async-start | bytes 12976128 | tf_op jit(solution)/shard_map/all_gather | solution.py:154
  401.1 14.6 %copy-start.14 = (f32[3,3,512]{2,1,0:T(4,128)S(1)}, f32[3,3,512]{2,1,0:T(4,128)}, u32[]{:S(2)}) copy-start(f32[3,3,512]{2,1,0:T(4,128)} %param.24) | copy-start | bytes 55300
  401.1 14.6 %copy-start.15 = (f32[32,128]{1,0:T(8,128)S(1)}, f32[32,128]{1,0:T(8,128)}, u32[]{:S(2)}) copy-start(f32[32,128]{1,0:T(8,128)} %param.25) | copy-start | bytes 49156
  412.1 1.2 copy-start.11
  413.5 124.3 %collective-permute-start.1 = (bf16[2,3,512]{0,2,1:T(8,128)(2,1)S(1)}, bf16[2,3,512]{0,2,1:T(8,128)(2,1)S(1)}, u32[]{:S(2)}, u32[]{:S(2)}) collective-permute-start(bf16[2,3,512]{0,2,1:T(8,128)(2,1)S(1)} %bitcast.243), channel_id=1, source_target_pairs={{0,8},{8,16},{16,24},{24,32},{32,40},{40,48},{48,56},{56,64},{64,7... | collective-permute-start | bytes 18440 | tf_op jit(solution)/shard_map/ppermute | solution.py:13
  541.4 9.9 %copy-start.3 = (f32[512,3,512]{0,2,1:T(8,128)}, f32[512,3,512]{0,2,1:T(8,128)S(1)}, u32[]{:S(2)}) copy-start(f32[512,3,512]{0,2,1:T(8,128)S(1)} %fusion.2) | copy-start | bytes 9437188
  541.6 9.0 %collective-permute-start.2 = (bf16[128,512]{0,1:T(8,128)(2,1)S(1)}, bf16[128,512]{0,1:T(8,128)(2,1)S(1)}, u32[]{:S(2)}, u32[]{:S(2)}) collective-permute-start(bf16[128,512]{0,1:T(8,128)(2,1)S(1)} %slice_bitcast_fusion.6), channel_id=1, source_target_pairs={{0,8},{8,16},{16,24},{24,32},{32,40},{40,48},{48,56},{56,64},{64,7... | collective-permute-start | bytes 393224 | tf_op jit(solution)/shard_map/ppermute | solution.py:13
  552.1 2.2 copy-start.2
  554.7 0.9 copy-start.21
  554.8 4.4 copy-start.1
Sparse Core Ops, SparseCore 0:
  13.9 62.3 all-gather.4
  78.1 57.5 all-gather.6
  198.3 101.6 all-gather.8
  301.6 99.4 all-gather.10
where the time goes:
time: 568 us; the launch traced here: 566 us
  waiting for transfers between devices  256 us (45%)
  local copies, waits for them, and re-layouts  198 us (35%)
  other arithmetic  35.1 us (6%)
  blocking collectives  29.8 us (5%)
  matrix products  24.8 us (4%)
  between operations  13.8 us (2%)
  starting transfers between devices  7.75 us (1%)
    gather x2, local copies, waits for them, and re-layouts, local(): medium_group_filter[:, jnp.clip(tap_delay, 0, tap_count - 1)]  120 us
    all_gather x1, waiting for transfers between devices, local(): piece = lax.all_gather(medium_weight, 'ctx', axis=0, tiled=True)  101 us
    all_gather x1, waiting for transfers between devices, local(): features = lax.all_gather(normed, 'ch', axis=1, tiled=True)  101 us
    gather x2, local copies, waits for them, and re-layouts, local(): kernel[:, jnp.clip(lag, 0, tap_count - 1)]  60 us
    all_gather x2, waiting for transfers between devices, carried_in(): pieces = jax.tree.map(lambda part: lax.all_gather(part, axis), value)  42.2 us
    psum x1, blocking collectives, local(): squares = lax.psum(jnp.sum(middle_wide * middle_wide, axis=1), 'ch')  29.8 us
    select_n x31, other arithmetic, turn(): jnp.where(position < mine, new, old)  24.4 us
    ppermute x3, waiting for transfers between devices, from_behind(): return lax.ppermute(x, axis, pairs)  12 us
  transfers between devices with their start and end apart: 7, of which 5 were waited for; matrix products, arithmetic and copies ran while one was open for 35% of the time, Pallas kernels for 0%

commit v1 on v0

--- a/solution.py
+++ b/solution.py
@@ -151,7 +151,16 @@
     scale = lax.rsqrt(squares / MODEL_WIDTH + epsilon)
     normed = (middle_wide * scale[:, None] * medium_gain.astype(jnp.float32)).astype(jnp.bfloat16)
     features = lax.all_gather(normed, "ch", axis=1, tiled=True)
-    piece = lax.all_gather(medium_weight, "ctx", axis=0, tiled=True)
+    draft_area = lambda w_in: jnp.concatenate(
+        lax.all_to_all(
+            jnp.stack([w_in for _ in range(lax.axis_size("ctx"))]),
+            axis_name="ctx",
+            split_axis=0,
+            concat_axis=0,
+        ),
+        0,
+    )
+    piece = draft_area(medium_weight)
     projected = jnp.dot(
         features, piece.reshape(piece.shape[0], 3 * channels), preferred_element_type=jnp.float32
     )

time: 568 us -> 710 us (1.25)
  waiting for transfers between devices: 256 us -> 364 us
  local copies, waits for them, and re-layouts: 198 us -> 221 us
  starting transfers between devices: 7.75 us -> 16.4 us
    ppermute x3, waiting for transfers between devices: 12 us -> 211 us  [from_behind(): return lax.ppermute(x, axis, pairs)]
    all_gather x1 -> x0, waiting for transfers between devices: 101 us -> none  [local(): piece = lax.all_gather(medium_weight, 'ctx', axis=0, tiled=True)]
    all_gather x2, waiting for transfers between devices: 42.2 us -> 58.1 us  [carried_in(): pieces = jax.tree.map(lambda part: lax.all_gather(part, axis), value)]
    all_to_all x0 -> x1, local copies, waits for them, and re-layouts: none -> 14.5 us  [local(): lax.all_to_all(jnp.stack([w_in for _ in range(lax.axis_size('ctx'))]), ax...]
    all_to_all x0 -> x1, starting transfers between devices: none -> 9.32 us  [local(): lax.all_to_all(jnp.stack([w_in for _ in range(lax.axis_size('ctx'))]), ax...]
    another operation x0 -> x1, local copies, waits for them, and re-layouts: none -> 7.62 us  [local(): jnp.stack([w_in for _ in range(lax.axis_size('ctx'))])]
  transfers between devices with their start and end apart: 7 -> 7, of which waited for: 5 -> 4; matrix products, arithmetic and copies ran while one was open for 35% -> 35% of each run, Pallas kernels for 0% -> 0%
where the time goes in v1:
time: 710 us; the launch traced here: 707 us
  waiting for transfers between devices  364 us (51%)
  local copies, waits for them, and re-layouts  221 us (31%)
  other arithmetic  35.1 us (5%)
  blocking collectives  29.8 us (4%)
  matrix products  26.9 us (4%)
  starting transfers between devices  16.4 us (2%)
  between operations  13.8 us (2%)
    ppermute x3, waiting for transfers between devices, from_behind(): return lax.ppermute(x, axis, pairs)  211 us
    gather x2, local copies, waits for them, and re-layouts, local(): medium_group_filter[:, jnp.clip(tap_delay, 0, tap_count - 1)]  121 us
    all_gather x1, waiting for transfers between devices, local(): features = lax.all_gather(normed, 'ch', axis=1, tiled=True)  94.2 us
    gather x2, local copies, waits for them, and re-layouts, local(): kernel[:, jnp.clip(lag, 0, tap_count - 1)]  60.3 us
    all_gather x2, waiting for transfers between devices, carried_in(): pieces = jax.tree.map(lambda part: lax.all_gather(part, axis), value)  58.1 us
    psum x1, blocking collectives, local(): squares = lax.psum(jnp.sum(middle_wide * middle_wide, axis=1), 'ch')  29.8 us
    select_n x31, other arithmetic, turn(): jnp.where(position < mine, new, old)  24.4 us
    all_to_all x1, local copies, waits for them, and re-layouts, local(): lax.all_to_all(jnp.stack([w_in for _ in range(lax.axis_size('ctx'))]), ax...  14.5 us
  transfers between devices with their start and end apart: 7, of which 4 were waited for; matrix products, arithmetic and copies ran while one was open for 35% of the time, Pallas kernels for 0%

profile of v1, /device:TPU:8, one launch (start us, length us, event | category | flops | bytes accessed | tf_op | source)
XLA Modules:
  0.0 707.4 jit_solution(4822329252907276250)
XLA Ops:
  6.5 1.3 copy.114
  7.8 7.6 %stack.17 = bf16[32,128,3,512]{1,3,2,0:T(8,128)(2,1)} broadcast(bf16[128,3,512]{0,2,1:T(8,128)(2,1)S(1)} %copy.114), dimensions={1,2,3} | broadcast | bytes 12976128 | tf_op jit(solution)/shard_map/stack | solution.py:156
  15.4 9.3 %all-to-all-start = ((bf16[32,128,3,512]{1,3,2,0:T(8,128)(2,1)}), bf16[32,128,3,512]{1,3,2,0:T(8,128)(2,1)}, u32[]{:S(2)}, u32[]{:S(2)}) async-start(bf16[32,128,3,512]{1,3,2,0:T(8,128)(2,1)} %stack.17), calls=%async_computation | async-start | bytes 25165824 | tf_op jit(solution)/shard_map/all_to_all | solution.py:155
  24.8 1.6 copy.94
  26.5 2.5 convolution_convert_fusion
  28.9 1.2 copy-done.10
  30.4 2.0 collective-permute-start
  33.8 1.7 copy.96
  35.7 205.2 %collective-permute-done = bf16[2,3,512]{0,2,1:T(8,128)(2,1)S(1)} collective-permute-done((bf16[2,3,512]{0,2,1:T(8,128)(2,1)S(1)}, bf16[2,3,512]{0,2,1:T(8,128)(2,1)S(1)}, u32[]{:S(2)}, u32[]{:S(2)}) %collective-permute-start) | collective-permute-done | bytes 6176 | tf_op jit(solution)/shard_map/ppermute | solution.py:13
  240.9 0.9 maximum_convert_fusion
  241.8 2.8 fusion.7
  246.5 0.9 copy-done.5
  248.8 54.8 %gather_fusion = f32[16384,32]{1,0:T(8,128)} fusion(f32[32,128]{0,1:T(8,128)S(1)} %copy.99, s32[16384]{0:T(1024)S(1)} %fusion.97), kind=kCustom, calls=%fused_computation | custom fusion | bytes 4259840 | tf_op jit(solution)/shard_map/gather | solution.py:118
  303.6 5.5 copy.100
  309.2 1.7 fusion.50
  310.9 1.4 fusion.32
  312.3 58.1 %all-gather.6.cloned.1.call-done = f32[32,16,512]{2,1,0:T(8,128)} async-done(((f32[1,16,512]{2,1,0:T(8,128)}), f32[32,16,512]{2,1,0:T(8,128)}) %all-gather.6.cloned.1.call-update) | async-done | bytes 1048592 | tf_op jit(solution)/shard_map/all_gather | solution.py:18
  370.4 25.2 %while.14 = (s32[]{:T(128)}, f32[16,512]{1,0:T(8,128)S(1)}, s32[]{:T(128)}, f32[32,16,512]{2,1,0:T(8,128)}, f32[32,16,512]{2,1,0:T(8,128)}, /*index=5*/s32[]{:T(128)}, s32[]{:T(128)}) while((s32[]{:T(128)}, f32[16,512]{1,0:T(8,128)S(1)}, s32[]{:T(128)}, f32[32,16,512]{2,1,0:T(8,128)}, f32[32,16,512]{2,1,0:T(8,128)}, ...), condition=%wide.region_3.4_spmd.clone, body=%wide.region_2.3_spmd.clone.sunk | while | flops 32772 | bytes 131173 | solution.py:27
  371.3 0.8 fusion.115
  372.1 0.8 fusion.115
  372.9 0.8 fusion.115
  373.7 0.8 fusion.115
  374.5 0.8 fusion.115
  375.3 0.8 fusion.115
  376.1 0.8 fusion.115
  376.9 0.8 fusion.115
  377.8 0.8 fusion.115
  378.6 0.8 fusion.115
  379.4 0.8 fusion.115
  380.2 0.8 fusion.115
  381.0 0.8 fusion.115
  381.8 0.8 fusion.115
  382.6 0.8 fusion.115
  383.4 0.8 fusion.115
  384.2 0.8 fusion.115
  385.1 0.8 fusion.115
  385.9 0.8 fusion.115
  386.7 0.8 fusion.115
  387.5 0.8 fusion.115
  388.3 0.8 fusion.115
  389.1 0.8 fusion.115
  389.9 0.8 fusion.115
  390.7 0.8 fusion.115
  391.6 0.8 fusion.115
  395.7 1.3 fusion.95
  397.0 1.1 fusion.46
  399.5 2.6 fusion.34
  402.1 29.8 %psum.7 = f32[512]{0:T(512)S(1)} all-reduce(f32[512]{0:T(512)S(1)} %get-tuple-element.144), channel_id=1, replica_groups=mesh['ctx'=32,'ch'=8] {'ch'}, use_global_device_ids=true, to_apply=%region_5.6 | all-reduce | flops 512 | bytes 4096 | tf_op jit(solution)/shard_map/psum | solution.py:150
  431.9 0.9 fusion.36
  433.0 14.5 %copy.115 = bf16[32,128,3,512]{1,0,3,2:T(8,128)(2,1)} copy(bf16[32,128,3,512]{1,3,2,0:T(8,128)(2,1)} %all-to-all-done) | data formatting | bytes 25165824 | tf_op jit(solution)/shard_map/all_to_all | solution.py:155
  447.6 94.2 %all-gather.8.cloned.1.call-done = bf16[512,4096]{0,1:T(8,128)(2,1)} async-done(((bf16[512,512]{0,1:T(8,128)(2,1)}), bf16[512,4096]{0,1:T(8,128)(2,1)}) %all-gather.8.cloned.1.call-update) | async-done | bytes 4194320 | tf_op jit(solution)/shard_map/all_gather | solution.py:153
  541.8 11.5 %fusion.9 = bf16[512,1536]{1,0:T(8,128)(2,1)S(1)} fusion(bf16[512,4096]{0,1:T(8,128)(2,1)} %all-gather.8.cloned.1.call-done, bf16[192,8,32,128]{3,2,1,0:T(8,128)(2,1)} %bitcast.236), kind=kOutput, calls=%fused_computation.21 | convolution fusion | flops 6443237376 | bytes 18350080 | tf_op jit(solution)/shard_map/dot_general | solution.py:164
  553.3 1.2 copy-done.11
  554.8 2.1 collective-permute-start.1
  557.0 109.0 %gather_fusion.1 = f32[32768,32]{1,0:T(8,128)} fusion(f32[32,128]{0,1:T(8,128)S(1)} %copy.120, s32[32768]{0:T(1024)S(1)} %fusion.84), kind=kCustom, calls=%fused_computation.1 | custom fusion | bytes 8519680 | tf_op jit(solution)/shard_map/gather | solution.py:181
  666.1 11.7 %copy.121 = f32[256,128,32]{1,0,2:T(8,128)} copy(f32[256,128,32]{2,1,0:T(8,128)} %bitcast.234) | data formatting | bytes 8388608 | tf_op jit(solution)/shard_map/gather | solution.py:181
  677.8 1.7 copy.117
  679.5 0.9 maximum_convert_fusion.1
  680.4 2.8 fusion.5
  683.4 2.6 collective-permute-start.2
  686.1 6.2 collective-permute-done.2
  694.5 1.5 copy-done.2
  697.4 2.4 fusion.37
  699.9 1.0 copy.124
  (105 shorter events, 14.8 us)
Async XLA Ops:
  6.5 302.7 %copy-start = (bf16[512,512]{1,0:T(8,128)(2,1)S(1)}, bf16[512,512]{1,0:T(8,128)(2,1)}, u32[]{:S(2)}) copy-start(bf16[512,512]{1,0:T(8,128)(2,1)} %param.16) | copy-start | bytes 1572868
  15.4 9.4 %copy-start.12 = (bf16[512,3,512]{2,0,1:T(8,128)(2,1)S(1)}, bf16[512,3,512]{2,0,1:T(8,128)(2,1)}, u32[]{:S(2)}) copy-start(bf16[512,3,512]{2,0,1:T(8,128)(2,1)} %param.17) | copy-start | bytes 4718596
  15.4 417.6 %all-to-all-start = ((bf16[32,128,3,512]{1,3,2,0:T(8,128)(2,1)}), bf16[32,128,3,512]{1,3,2,0:T(8,128)(2,1)}, u32[]{:S(2)}, u32[]{:S(2)}) async-start(bf16[32,128,3,512]{1,3,2,0:T(8,128)(2,1)} %stack.17), calls=%async_computation | async-start | bytes 25165824 | tf_op jit(solution)/shard_map/all_to_all | solution.py:155
  24.8 1.7 copy-start.19
  24.8 287.5 %all-gather.4.cloned.1.call-start = ((), (), s32[]{:S(2)}) async-start(), calls=%async_computation.1 | async-start | bytes 1081344 | tf_op jit(solution)/shard_map/all_gather | solution.py:18
  26.4 6.0 copy-start.16
  26.4 6.0 copy-start.17
  26.4 7.0 copy-start.18
  26.4 7.3 %copy-start.13 = (f32[3,3,512]{2,1,0:T(4,128)S(1)}, f32[3,3,512]{2,1,0:T(4,128)}, u32[]{:S(2)}) copy-start(f32[3,3,512]{2,1,0:T(4,128)} %param.18) | copy-start | bytes 55300
  28.9 1.2 copy-start.10
  30.4 210.5 %collective-permute-start = (bf16[2,3,512]{0,2,1:T(8,128)(2,1)S(1)}, bf16[2,3,512]{0,2,1:T(8,128)(2,1)S(1)}, u32[]{:S(2)}, u32[]{:S(2)}) collective-permute-start(bf16[2,3,512]{0,2,1:T(8,128)(2,1)S(1)} %bitcast.250), channel_id=1, source_target_pairs={{0,8},{8,16},{16,24},{24,32},{32,40},{40,48},{48,56},{56,64},{64,7... | collective-permute-start | bytes 18440 | tf_op jit(solution)/shard_map/ppermute | solution.py:13
  33.4 337.0 %all-gather.6.cloned.1.call-start = ((), (), s32[]{:S(2)}) async-start(), calls=%async_computation.2 | async-start | bytes 1081344 | tf_op jit(solution)/shard_map/all_gather | solution.py:18
  244.6 1.8 copy-start.4
  244.7 0.9 copy-start.8
  246.4 1.0 copy-start.5
  248.1 293.7 %all-gather.8.cloned.1.call-start = ((), (), s32[]{:S(2)}) async-start(), calls=%async_computation.3 | async-start | bytes 4718592 | tf_op jit(solution)/shard_map/all_gather | solution.py:153
  303.6 5.5 copy-start.22
  395.7 2.4 copy-start.7
  398.2 1.2 copy-start.6
  398.2 1.3 copy-start.9
  398.2 1.3 copy-start.20
  541.8 15.1 %copy-start.14 = (f32[3,3,512]{2,1,0:T(4,128)S(1)}, f32[3,3,512]{2,1,0:T(4,128)}, u32[]{:S(2)}) copy-start(f32[3,3,512]{2,1,0:T(4,128)} %param.24) | copy-start | bytes 55300
  541.8 15.2 %copy-start.15 = (f32[32,128]{1,0:T(8,128)S(1)}, f32[32,128]{1,0:T(8,128)}, u32[]{:S(2)}) copy-start(f32[32,128]{1,0:T(8,128)} %param.25) | copy-start | bytes 49156
  553.3 1.2 copy-start.11
  554.8 124.8 %collective-permute-start.1 = (bf16[2,3,512]{0,2,1:T(8,128)(2,1)S(1)}, bf16[2,3,512]{0,2,1:T(8,128)(2,1)S(1)}, u32[]{:S(2)}, u32[]{:S(2)}) collective-permute-start(bf16[2,3,512]{0,2,1:T(8,128)(2,1)S(1)} %bitcast.251), channel_id=1, source_target_pairs={{0,8},{8,16},{16,24},{24,32},{32,40},{40,48},{48,56},{56,64},{64,7... | collective-permute-start | bytes 18440 | tf_op jit(solution)/shard_map/ppermute | solution.py:13
  683.2 9.9 %copy-start.3 = (f32[512,3,512]{0,2,1:T(8,128)}, f32[512,3,512]{0,2,1:T(8,128)S(1)}, u32[]{:S(2)}) copy-start(f32[512,3,512]{0,2,1:T(8,128)S(1)} %fusion.5) | copy-start | bytes 9437188
  683.4 9.0 %collective-permute-start.2 = (bf16[128,512]{0,1:T(8,128)(2,1)S(1)}, bf16[128,512]{0,1:T(8,128)(2,1)S(1)}, u32[]{:S(2)}, u32[]{:S(2)}) collective-permute-start(bf16[128,512]{0,1:T(8,128)(2,1)S(1)} %slice_bitcast_fusion.6), channel_id=1, source_target_pairs={{0,8},{8,16},{16,24},{24,32},{32,40},{40,48},{48,56},{56,64},{64,7... | collective-permute-start | bytes 393224 | tf_op jit(solution)/shard_map/ppermute | solution.py:13
  693.8 2.2 copy-start.2
  696.5 0.9 copy-start.21
  696.5 4.4 copy-start.1
Sparse Core Ops, SparseCore 0:
  33.5 112.5 all-gather.3
  248.2 122.1 all-gather.5
  433.0 108.7 all-gather.7
